TPU v7x, 128 devices: a whole 4x4x4 slice. The times are simulated.
128 devices in a mesh: elem: 16 (over z_hi, y, core), mode: 8 (over x, z_lo).
Axes of the slice: x: 4, y: 4, z: 4 (z_hi: 2, z_lo: 2; z = z_hi * 2 + z_lo), core: 2. Of those that a mesh axis runs over, the one named last changes fastest.
Arguments:
- iterate: float32 [480, 16384], P('mode', 'elem'), may hold values from -0.75 to 0.75
- newton_residual: float32 [480, 16384], P('mode', 'elem'), may hold values from -6 to 6
- inverse_blocks: float32 [64, 16384], P(None, 'elem'), may hold values from -0.15 to 2
- basis_values: bfloat16 [1024, 480], replicated, may hold values from -4 to 4, as said below
- triple_blocks: bfloat16 [8, 60, 20160], P('mode', None, 'elem'), may hold values from -0.375 to 0.375
- block_columns: int32 [8, 4], P('mode'), may hold values from 0 to 7, as said below
- neighbour_ids: int32 [256, 6], P('elem'), may hold values from 0 to 15, as said below
Outputs:
- correction: float32 [480, 16384], P('mode', 'elem')
- linear_residual: float32 [480, 16384], P('mode', 'elem')
Inputs may be any that keep to these rules, and one draw needn't show every extreme that they name: `neighbour_ids`: columns 0 to 3 give the neighbour across the -y, +y, -z, +z faces within the element's own block of 16 elements; columns 4 and 5 the neighbour across the -x and +x faces within the previous and the next block, cyclically. Neighbours are mutual across opposite faces. `block_columns`: row b names 4 different block columns; the first is b. `basis_values`: column 0 holds ones, the constant mode.
All inputs are finite; a program needn't handle non-finite values.
Results may differ from a plain program's by a relative error of at most 0.0039.
Values may be sent and summed in bfloat16 or wider, within the bound.
No kernel may reach another device: no remote copies, remote signals or barrier semaphores. Data moves between devices by JAX's collectives and lax.ppermute only.
A program may use at most 128 MiB of HBM per device.

v0:
```python
import math
import jax
import jax.numpy as jnp
import numpy as np
from jax import lax
from jax.sharding import PartitionSpec as P

K = 84
S = 1024
ITERS = 2
MB = 60
GROWTH = 0.5
TIME_STEP = 0.03
LIFT_SCALE = 6.0
PENALTY = 3.0
RELAX_WEIGHT = 0.8
SLAB_ENTRIES = 6291456
FACE_AXIS = (1, 1, 2, 2, 0, 0)
FACE_SIGN = (-1.0, 1.0, -1.0, 1.0, -1.0, 1.0)
FACE_OPPOSITE = (1, 0, 3, 2, 5, 4)


def padded(block, sides, width):
    for axis, dim in sides:
        count = lax.axis_size(axis)
        forward = [(i, i + 1) for i in range(count - 1)]
        forward.append((count - 1, 0))
        backward = [(target, source) for source, target in forward]
        low = lax.ppermute(
            lax.slice_in_dim(block, block.shape[dim] - width, None, axis=dim), axis, forward
        )
        high = lax.ppermute(lax.slice_in_dim(block, 0, width, axis=dim), axis, backward)
        block = jnp.concatenate([low, block, high], axis=dim)
    return block


def line_derivative():
    inward = 1.0 / math.sqrt(5.0)
    points = np.array([-1.0, -inward, inward, 1.0])
    legendre = (5.0 * points**3 - 3.0 * points) / 2.0
    matrix = np.zeros((4, 4))
    for source in range(4):
        for target in range(4):
            if source != target:
                matrix[source, target] = legendre[source] / (
                    legendre[target] * (points[source] - points[target])
                )
    matrix[0, 0] = -3.0
    matrix[3, 3] = 3.0
    return matrix


def direction_tables():
    line_matrix = line_derivative()
    identity = np.eye(4)
    singles = [
        np.kron(np.kron(line_matrix, identity), identity),
        np.kron(np.kron(identity, line_matrix), identity),
        np.kron(np.kron(identity, identity), line_matrix),
    ]
    return [np.kron(np.eye(2), single).T.astype(np.float32) for single in singles]


def face_nodes():
    layout = np.arange(64).reshape(4, 4, 4)
    return np.stack(
        [
            layout[:, 0, :].ravel(),
            layout[:, 3, :].ravel(),
            layout[:, :, 0].ravel(),
            layout[:, :, 3].ravel(),
            layout[0].ravel(),
            layout[3].ravel(),
        ]
    )


def embed_table():
    nodes_list = face_nodes()
    table_out = np.zeros((96, 64), np.float32)
    for face_index in range(6):
        for within in range(16):
            table_out[face_index * 16 + within, nodes_list[face_index, within]] = 1.0
    return table_out


def volume_derivative(field, single):
    modes_count = field.shape[0]
    paired = field.reshape(-1, 128)
    return jnp.dot(paired, single, precision=lax.Precision.HIGHEST).reshape(modes_count, -1)


def apply_inverse(field, inverse_blocks):
    modes_count = field.shape[0]
    shaped = field.reshape(modes_count, -1, 64)
    inverse = inverse_blocks.reshape(64, -1, 64)
    return jnp.einsum("mer,req->meq", shaped, inverse, precision=lax.Precision.HIGHEST).reshape(
        modes_count, -1
    )


def own_traces(values, flux_fields, face_index, axis_index):
    nodes_list = face_nodes()
    return (
        values[:, :, nodes_list[face_index]],
        flux_fields[axis_index][:, :, nodes_list[face_index]],
    )


def lift_terms(values, flux_fields, sources, near_ids, embed_matrix):
    pieces = []
    for face_index in range(6):
        own_values, own_fluxes = own_traces(values, flux_fields, face_index, FACE_AXIS[face_index])
        near_values = jnp.take(sources[face_index][0], near_ids[:, face_index], axis=1)
        near_fluxes = jnp.take(sources[face_index][1], near_ids[:, face_index], axis=1)
        pieces.append(
            LIFT_SCALE
            * (
                0.5 * FACE_SIGN[face_index] * (near_fluxes - own_fluxes)
                + PENALTY * (near_values - own_values)
            )
        )
    joined = jnp.concatenate(pieces, axis=2)
    return jnp.einsum("mef,fq->meq", joined, embed_matrix, precision=lax.Precision.HIGHEST)


def largest_divisor(number, ceiling):
    found = 1
    for candidate in range(1, ceiling + 1):
        if number % candidate == 0:
            found = candidate
    return found


def select_blocks(gathered, block_columns):
    pieces_list = [
        lax.dynamic_slice_in_dim(gathered, block_columns[0, stored] * MB, MB, 1)
        for stored in range(block_columns.shape[1])
    ]
    per_row = [jnp.concatenate(pieces_list, axis=1)]
    return jnp.stack(per_row)


def add_slab(running, blocks_piece, selected, coeff_terms, first_row):
    row_count = blocks_piece.shape[2] // K
    ceiling_rows = max(8, SLAB_ENTRIES // (3 * K * selected.shape[0] * selected.shape[3]))
    slab_rows = largest_divisor(row_count, ceiling_rows)
    spread = coeff_terms.astype(jnp.float32)

    def one_slab(slab_index, current):
        offset = slab_index * slab_rows
        picked = lax.dynamic_slice_in_dim(selected, first_row + offset, slab_rows, 2)
        expanded = (
            picked.astype(jnp.float32)[:, :, :, None, :] * spread[None, None, None, :, :]
        ).astype(jnp.bfloat16)
        expanded = expanded.reshape(picked.shape[0], 3, slab_rows * K, picked.shape[3])
        weights = lax.dynamic_slice_in_dim(blocks_piece, offset * K, slab_rows * K, 2)
        return current + jnp.einsum(
            "bil,bcln->cbin", weights, expanded, preferred_element_type=jnp.float32
        )

    return lax.fori_loop(0, row_count // slab_rows, one_slab, running)


def apply_jacobian(
    iterate_now, coeff_terms, triple_blocks, block_columns, neighbour_ids, tables, embed_matrix
):
    modes_local, nodes_count = iterate_now.shape
    gradients = jnp.stack([volume_derivative(iterate_now, single) for single in tables]).astype(
        jnp.bfloat16
    )
    gathered = lax.all_gather(gradients, "mode", axis=1, tiled=True)
    selected = select_blocks(gathered, block_columns)
    empty_sum = jnp.zeros((3, block_columns.shape[0], MB, nodes_count), jnp.float32)
    running = add_slab(
        empty_sum,
        lax.all_gather(triple_blocks, "elem", axis=2, tiled=True),
        selected,
        coeff_terms,
        jnp.int32(0) // K,
    )
    fluxes = running.astype(jnp.bfloat16).reshape(3, modes_local, nodes_count)
    values = iterate_now.reshape(modes_local, -1, 64)
    elements = values.shape[1]
    flux_fields = fluxes.astype(jnp.float32).reshape(3, modes_local, elements, 64)
    outward = jnp.stack(
        [
            jnp.stack(own_traces(values, flux_fields, 4, 0)),
            jnp.stack(own_traces(values, flux_fields, 5, 0)),
        ]
    )
    bordered = padded(outward.reshape(2, 2, modes_local, elements * 16), (("elem", 0),), 1)
    previous_side = bordered[0].reshape(2, modes_local, elements, 16)
    next_side = bordered[3].reshape(2, modes_local, elements, 16)
    sources = [
        own_traces(values, flux_fields, FACE_OPPOSITE[face_index], FACE_AXIS[face_index])
        for face_index in range(4)
    ]
    sources = sources + [(previous_side[0], previous_side[1]), (next_side[0], next_side[1])]
    lifted = lift_terms(values, flux_fields, sources, neighbour_ids, embed_matrix)
    divergence = lifted.reshape(modes_local, -1)
    for axis_index in range(3):
        divergence = divergence + volume_derivative(
            flux_fields[axis_index].reshape(modes_local, -1), tables[axis_index]
        )
    return iterate_now - TIME_STEP * divergence


def per_device(
    iterate,
    newton_residual,
    inverse_blocks,
    basis_values,
    triple_blocks,
    block_columns,
    neighbour_ids,
):
    tables = [jnp.asarray(single) for single in direction_tables()]
    embed_matrix = jnp.asarray(embed_table())
    modes_local = iterate.shape[0]
    low_state = iterate.astype(jnp.bfloat16)
    offset = lax.axis_index("mode") * modes_local
    local_basis = lax.dynamic_slice_in_dim(basis_values, offset, modes_local, 1)
    sampled = lax.psum_scatter(
        lax.dot_general(
            low_state, local_basis, (((0,), (1,)), ((), ())), preferred_element_type=jnp.float32
        ),
        "mode",
        scatter_dimension=0,
        tiled=True,
    )
    growth = jnp.exp(GROWTH * sampled)
    leading = basis_values[:, :K].astype(jnp.float32)
    node_terms = jnp.dot(growth, leading, precision=lax.Precision.HIGHEST) / S
    coeff_terms = lax.all_gather(node_terms.T.astype(jnp.bfloat16), "mode", axis=1, tiled=True)
    correction = apply_inverse(newton_residual, inverse_blocks)
    remainder = newton_residual
    for sweep_index in range(ITERS):
        applied = apply_jacobian(
            correction,
            coeff_terms,
            triple_blocks,
            block_columns,
            neighbour_ids,
            tables,
            embed_matrix,
        )
        remainder = newton_residual - applied
        correction = correction + RELAX_WEIGHT * apply_inverse(remainder, inverse_blocks)
    return (correction, remainder)


def solution(mesh):
    return jax.shard_map(
        per_device,
        mesh=mesh,
        in_specs=(
            P("mode", "elem"),
            P("mode", "elem"),
            P(None, "elem"),
            P(),
            P("mode", None, "elem"),
            P("mode", None),
            P("elem", None),
        ),
        out_specs=(P("mode", "elem"), P("mode", "elem")),
        check_vma=False,
    )
```

profile of v0, /device:TPU:34, one launch (start us, length us, event | category | flops | bytes accessed | tf_op | source)
XLA Modules:
  0.0 1195.9 jit_solution(10864782961386579404)
XLA Ops:
  42.5 49.8 %all-gather.6.cloned.1.call-done = bf16[1,60,20160]{1,0,2:T(2,128)(2,1)} async-done(((bf16[1,60,1260]{1,0,2:T(2,128)(2,1)}), bf16[1,60,20160]{1,0,2:T(2,128)(2,1)}) %all-gather.6.cloned.1.call-update) | async-done | bytes 2419216 | tf_op jit(solution)/shard_map/all_gather | solution.py:177
  92.3 20.8 %copy.469 = bf16[1,60,20160]{2,1,0:T(8,128)(2,1)} copy(bf16[1,60,20160]{1,0,2:T(2,128)(2,1)} %all-gather.6.cloned.1.call-done) | data formatting | bytes 4838400
  113.1 65.3 %all-gather.4.cloned.1.call-done = bf16[3,480,1024]{2,0,1:T(4,128)(2,1)} async-done(((bf16[3,60,1024]{2,0,1:T(4,128)(2,1)}), bf16[3,480,1024]{2,0,1:T(4,128)(2,1)}) %all-gather.4.cloned.1.call-update) | async-done | bytes 2949136 | tf_op jit(solution)/shard_map/all_gather | solution.py:172
  183.9 86.9 %reduce-scatter.2.cloned.1.call-done = f32[128,1024]{0,1:T(8,128)} async-done(((f32[1024,1024]{0,1:T(8,128)}), f32[128,1024]{0,1:T(8,128)}) %reduce-scatter.2.cloned.1.call-update) | async-done | bytes 524304 | tf_op jit(solution)/shard_map/reduce_scatter | solution.py:224
  272.3 22.7 %all_gather.14 = bf16[84,1024]{1,0:T(8,128)(2,1)S(1)} all-gather(bf16[84,128]{1,0:T(8,128)(2,1)S(1)} %fusion.9), channel_id=1, replica_groups=mesh['elem'=16,'mode'=8] {'mode'}, dimensions={1}, use_global_device_ids=true | all-gather | bytes 193536 | tf_op jit(solution)/shard_map/all_gather | solution.py:235
  295.1 332.9 %while.32 = (s32[]{:T(128)}, f32[3,1,60,1024]{3,2,0,1:T(8,128)S(1)}, bf16[1,3,240,1024]{3,2,1,0:T(8,128)(2,1)}, f32[84,1024]{1,0:T(8,128)S(1)}, bf16[1,60,20160]...) while((s32[]{:T(128)}, ...), condition=%wide.region_2.3_spmd.clone, body=%wide.region_1.2_spmd.clone.sunk | while | flops 756006912 | bytes 52363480 | solution.py:162
  305.5 15.8 %convert_element_type.114 = bf16[3,2016,1024]{2,1,0:T(8,128)(2,1)} reshape(bf16[3,24,84,1024]{3,2,1,0:T(8,128)(2,1)} %multiply_convert_fusion.4) | data formatting | bytes 24772608 | tf_op jit(solution)/shard_map/while/body/eval_jaxpr/convert_element_type | solution.py:155
  329.3 9.4 multiply_convert_fusion.4
  338.7 15.8 %convert_element_type.114 = bf16[3,2016,1024]{2,1,0:T(8,128)(2,1)} reshape(bf16[3,24,84,1024]{3,2,1,0:T(8,128)(2,1)} %multiply_convert_fusion.4) | data formatting | bytes 24772608 | tf_op jit(solution)/shard_map/while/body/eval_jaxpr/convert_element_type | solution.py:155
  362.6 9.4 multiply_convert_fusion.4
  372.0 15.8 %convert_element_type.114 = bf16[3,2016,1024]{2,1,0:T(8,128)(2,1)} reshape(bf16[3,24,84,1024]{3,2,1,0:T(8,128)(2,1)} %multiply_convert_fusion.4) | data formatting | bytes 24772608 | tf_op jit(solution)/shard_map/while/body/eval_jaxpr/convert_element_type | solution.py:155
  405.3 15.8 %convert_element_type.114 = bf16[3,2016,1024]{2,1,0:T(8,128)(2,1)} reshape(bf16[3,24,84,1024]{3,2,1,0:T(8,128)(2,1)} %multiply_convert_fusion.4) | data formatting | bytes 24772608 | tf_op jit(solution)/shard_map/while/body/eval_jaxpr/convert_element_type | solution.py:155
  429.1 9.4 multiply_convert_fusion.4
  438.6 15.8 %convert_element_type.114 = bf16[3,2016,1024]{2,1,0:T(8,128)(2,1)} reshape(bf16[3,24,84,1024]{3,2,1,0:T(8,128)(2,1)} %multiply_convert_fusion.4) | data formatting | bytes 24772608 | tf_op jit(solution)/shard_map/while/body/eval_jaxpr/convert_element_type | solution.py:155
  471.9 15.8 %convert_element_type.114 = bf16[3,2016,1024]{2,1,0:T(8,128)(2,1)} reshape(bf16[3,24,84,1024]{3,2,1,0:T(8,128)(2,1)} %multiply_convert_fusion.4) | data formatting | bytes 24772608 | tf_op jit(solution)/shard_map/while/body/eval_jaxpr/convert_element_type | solution.py:155
  505.2 15.8 %convert_element_type.114 = bf16[3,2016,1024]{2,1,0:T(8,128)(2,1)} reshape(bf16[3,24,84,1024]{3,2,1,0:T(8,128)(2,1)} %multiply_convert_fusion.4) | data formatting | bytes 24772608 | tf_op jit(solution)/shard_map/while/body/eval_jaxpr/convert_element_type | solution.py:155
  538.4 15.8 %convert_element_type.114 = bf16[3,2016,1024]{2,1,0:T(8,128)(2,1)} reshape(bf16[3,24,84,1024]{3,2,1,0:T(8,128)(2,1)} %multiply_convert_fusion.4) | data formatting | bytes 24772608 | tf_op jit(solution)/shard_map/while/body/eval_jaxpr/convert_element_type | solution.py:155
  571.8 15.8 %convert_element_type.114 = bf16[3,2016,1024]{2,1,0:T(8,128)(2,1)} reshape(bf16[3,24,84,1024]{3,2,1,0:T(8,128)(2,1)} %multiply_convert_fusion.4) | data formatting | bytes 24772608 | tf_op jit(solution)/shard_map/while/body/eval_jaxpr/convert_element_type | solution.py:155
  605.1 15.8 %convert_element_type.114 = bf16[3,2016,1024]{2,1,0:T(8,128)(2,1)} reshape(bf16[3,24,84,1024]{3,2,1,0:T(8,128)(2,1)} %multiply_convert_fusion.4) | data formatting | bytes 24772608 | tf_op jit(solution)/shard_map/while/body/eval_jaxpr/convert_element_type | solution.py:155
  716.7 68.9 %all-gather.8.cloned.1.call-done = bf16[3,480,1024]{2,0,1:T(4,128)(2,1)} async-done(((bf16[3,60,1024]{2,0,1:T(4,128)(2,1)}), bf16[3,480,1024]{2,0,1:T(4,128)(2,1)}) %all-gather.8.cloned.1.call-update) | async-done | bytes 2949136 | tf_op jit(solution)/shard_map/all_gather | solution.py:172
  791.1 333.3 %while.33 = (s32[]{:T(128)}, f32[3,1,60,1024]{3,2,0,1:T(8,128)S(1)}, bf16[1,3,240,1024]{3,2,1,0:T(8,128)(2,1)}, f32[84,1024]{1,0:T(8,128)S(1)}, bf16[1,60,20160]...) while((s32[]{:T(128)}, ...), condition=%wide.region_4.6_spmd.clone, body=%wide.region_3.5_spmd.clone.sunk | while | flops 756006912 | bytes 52363480 | solution.py:162
  801.9 15.8 %convert_element_type.116 = bf16[3,2016,1024]{2,1,0:T(8,128)(2,1)} reshape(bf16[3,24,84,1024]{3,2,1,0:T(8,128)(2,1)} %multiply_convert_fusion.5) | data formatting | bytes 24772608 | tf_op jit(solution)/shard_map/while/body/eval_jaxpr/convert_element_type | solution.py:155
  835.1 15.8 %convert_element_type.116 = bf16[3,2016,1024]{2,1,0:T(8,128)(2,1)} reshape(bf16[3,24,84,1024]{3,2,1,0:T(8,128)(2,1)} %multiply_convert_fusion.5) | data formatting | bytes 24772608 | tf_op jit(solution)/shard_map/while/body/eval_jaxpr/convert_element_type | solution.py:155
  868.4 15.8 %convert_element_type.116 = bf16[3,2016,1024]{2,1,0:T(8,128)(2,1)} reshape(bf16[3,24,84,1024]{3,2,1,0:T(8,128)(2,1)} %multiply_convert_fusion.5) | data formatting | bytes 24772608 | tf_op jit(solution)/shard_map/while/body/eval_jaxpr/convert_element_type | solution.py:155
  901.7 15.8 %convert_element_type.116 = bf16[3,2016,1024]{2,1,0:T(8,128)(2,1)} reshape(bf16[3,24,84,1024]{3,2,1,0:T(8,128)(2,1)} %multiply_convert_fusion.5) | data formatting | bytes 24772608 | tf_op jit(solution)/shard_map/while/body/eval_jaxpr/convert_element_type | solution.py:155
  935.0 15.8 %convert_element_type.116 = bf16[3,2016,1024]{2,1,0:T(8,128)(2,1)} reshape(bf16[3,24,84,1024]{3,2,1,0:T(8,128)(2,1)} %multiply_convert_fusion.5) | data formatting | bytes 24772608 | tf_op jit(solution)/shard_map/while/body/eval_jaxpr/convert_element_type | solution.py:155
  968.3 15.8 %convert_element_type.116 = bf16[3,2016,1024]{2,1,0:T(8,128)(2,1)} reshape(bf16[3,24,84,1024]{3,2,1,0:T(8,128)(2,1)} %multiply_convert_fusion.5) | data formatting | bytes 24772608 | tf_op jit(solution)/shard_map/while/body/eval_jaxpr/convert_element_type | solution.py:155
  1001.6 15.8 %convert_element_type.116 = bf16[3,2016,1024]{2,1,0:T(8,128)(2,1)} reshape(bf16[3,24,84,1024]{3,2,1,0:T(8,128)(2,1)} %multiply_convert_fusion.5) | data formatting | bytes 24772608 | tf_op jit(solution)/shard_map/while/body/eval_jaxpr/convert_element_type | solution.py:155
  1034.8 15.8 %convert_element_type.116 = bf16[3,2016,1024]{2,1,0:T(8,128)(2,1)} reshape(bf16[3,24,84,1024]{3,2,1,0:T(8,128)(2,1)} %multiply_convert_fusion.5) | data formatting | bytes 24772608 | tf_op jit(solution)/shard_map/while/body/eval_jaxpr/convert_element_type | solution.py:155
  1068.2 15.8 %convert_element_type.116 = bf16[3,2016,1024]{2,1,0:T(8,128)(2,1)} reshape(bf16[3,24,84,1024]{3,2,1,0:T(8,128)(2,1)} %multiply_convert_fusion.5) | data formatting | bytes 24772608 | tf_op jit(solution)/shard_map/while/body/eval_jaxpr/convert_element_type | solution.py:155
  1092.1 9.4 multiply_convert_fusion.5
  1101.5 15.8 %convert_element_type.116 = bf16[3,2016,1024]{2,1,0:T(8,128)(2,1)} reshape(bf16[3,24,84,1024]{3,2,1,0:T(8,128)(2,1)} %multiply_convert_fusion.5) | data formatting | bytes 24772608 | tf_op jit(solution)/shard_map/while/body/eval_jaxpr/convert_element_type | solution.py:155
  (453 shorter events, 509.5 us)
Async XLA Ops:
  7.2 85.1 %all-gather.6.cloned.1.call-start = ((), (), s32[]{:S(2)}) async-start(), calls=%async_computation.3 | async-start | bytes 10967040 | tf_op jit(solution)/shard_map/all_gather | solution.py:177
  9.4 169.0 %all-gather.4.cloned.1.call-start = ((), (), s32[]{:S(2)}) async-start(), calls=%async_computation.1 | async-start | bytes 4423680 | tf_op jit(solution)/shard_map/all_gather | solution.py:172
  16.3 254.5 %reduce-scatter.2.cloned.1.call-start = ((), (), s32[]{:S(2)}) async-start(), calls=%async_computation.2 | async-start | bytes 4718592 | tf_op jit(solution)/shard_map/reduce_scatter | solution.py:224
  20.1 765.5 %all-gather.8.cloned.1.call-start = ((), (), s32[]{:S(2)}) async-start(), calls=%async_computation.4 | async-start | bytes 4423680 | tf_op jit(solution)/shard_map/all_gather | solution.py:172
  26.8 603.3 %copy-start.60 = (s32[1024]{0:T(1024)}, s32[1024]{0:T(1024)S(1)}, u32[]{:S(2)}) copy-start(s32[1024]{0:T(1024)S(1)} %pad_clamp_fusion.3) | copy-start | bytes 12292
  29.1 603.0 %copy-start.59 = (s32[1024]{0:T(1024)}, s32[1024]{0:T(1024)S(1)}, u32[]{:S(2)}) copy-start(s32[1024]{0:T(1024)S(1)} %pad_clamp_fusion.5) | copy-start | bytes 12292
  30.0 602.7 %copy-start.62 = (s32[1024]{0:T(1024)}, s32[1024]{0:T(1024)S(1)}, u32[]{:S(2)}) copy-start(s32[1024]{0:T(1024)S(1)} %pad_clamp_fusion.7) | copy-start | bytes 12292
  33.3 605.1 %copy-start.63 = (s32[1024]{0:T(1024)}, s32[1024]{0:T(1024)S(1)}, u32[]{:S(2)}) copy-start(s32[1024]{0:T(1024)S(1)} %pad_clamp_fusion.11) | copy-start | bytes 12292
  34.1 79.0 %copy-start.4 = (f32[16,60,16]{0,1,2:T(8,128)}, f32[16,60,16]{0,1,2:T(8,128)S(1)}, u32[]{:S(2)}) copy-start(f32[16,60,16]{0,1,2:T(8,128)S(1)} %copy.475) | copy-start | bytes 184324
  34.8 634.9 %copy-start.72 = (pred[16]{0:T(512)(128)(4,1)}, pred[16]{0:T(512)(128)(4,1)S(1)}, u32[]{:S(2)}) copy-start(pred[16]{0:T(512)(128)(4,1)S(1)} %get-tuple-element.439) | copy-start | bytes 52
  34.8 637.0 %copy-start.74 = (pred[16]{0:T(512)(128)(4,1)}, pred[16]{0:T(512)(128)(4,1)S(1)}, u32[]{:S(2)}) copy-start(pred[16]{0:T(512)(128)(4,1)S(1)} %get-tuple-element.441) | copy-start | bytes 52
  34.8 647.6 %copy-start.68 = (pred[16]{0:T(512)(128)(4,1)}, pred[16]{0:T(512)(128)(4,1)S(1)}, u32[]{:S(2)}) copy-start(pred[16]{0:T(512)(128)(4,1)S(1)} %get-tuple-element.395) | copy-start | bytes 52
  34.9 649.9 %copy-start.70 = (pred[16]{0:T(512)(128)(4,1)}, pred[16]{0:T(512)(128)(4,1)S(1)}, u32[]{:S(2)}) copy-start(pred[16]{0:T(512)(128)(4,1)S(1)} %get-tuple-element.443) | copy-start | bytes 52
  34.9 610.0 %copy-start.65 = (s32[1024]{0:T(1024)}, s32[1024]{0:T(1024)S(1)}, u32[]{:S(2)}) copy-start(s32[1024]{0:T(1024)S(1)} %pad_clamp_fusion.4) | copy-start | bytes 12292
  36.3 611.2 %copy-start.64 = (s32[1024]{0:T(1024)}, s32[1024]{0:T(1024)S(1)}, u32[]{:S(2)}) copy-start(s32[1024]{0:T(1024)S(1)} %pad_clamp_fusion.6) | copy-start | bytes 12292
  38.7 611.2 %copy-start.61 = (s32[1024]{0:T(1024)}, s32[1024]{0:T(1024)S(1)}, u32[]{:S(2)}) copy-start(s32[1024]{0:T(1024)S(1)} %pad_clamp_fusion.8) | copy-start | bytes 12292
  41.1 612.1 %copy-start.66 = (s32[1024]{0:T(1024)}, s32[1024]{0:T(1024)S(1)}, u32[]{:S(2)}) copy-start(s32[1024]{0:T(1024)S(1)} %pad_clamp_fusion.10) | copy-start | bytes 12292
  642.3 31.6 %collective-permute-start.1 = (f32[1,2,60,256]{2,3,1,0:T(8,128)}, f32[1,2,60,256]{2,3,1,0:T(8,128)}, u32[]{:S(2)}, u32[]{:S(2)}) collective-permute-start(f32[1,2,60,256]{2,3,1,0:T(8,128)} %pad_maximum_fusion.3), channel_id=1, source_target_pairs={{8,0},{16,8},{24,16},{32,24},{40,32},{48,40},{56,48},{64,56},{72,6... | collective-permute-start | bytes 368648 | tf_op jit(solution)/shard_map/ppermute | solution.py:32
  644.1 34.1 %collective-permute-start = (f32[1,2,60,256]{2,3,1,0:T(8,128)}, f32[1,2,60,256]{2,3,1,0:T(8,128)}, u32[]{:S(2)}, u32[]{:S(2)}) collective-permute-start(f32[1,2,60,256]{2,3,1,0:T(8,128)} %pad_maximum_fusion.2), channel_id=1, source_target_pairs={{0,8},{8,16},{16,24},{24,32},{32,40},{40,48},{48,56},{56,64},{64,7... | collective-permute-start | bytes 368648 | tf_op jit(solution)/shard_map/ppermute | solution.py:29
  646.2 18.5 %copy-start.3 = (f32[16,60,16]{0,1,2:T(8,128)S(1)}, f32[16,60,16]{0,1,2:T(8,128)}, u32[]{:S(2)}) copy-start(f32[16,60,16]{0,1,2:T(8,128)} %copy.483) | copy-start | bytes 184324
  646.2 18.6 %copy-start.76 = (pred[16]{0:T(512)(128)(4,1)S(1)}, pred[16]{0:T(512)(128)(4,1)}, u32[]{:S(2)}) copy-start(pred[16]{0:T(512)(128)(4,1)} %get-tuple-element.435) | copy-start | bytes 52
  649.9 17.4 %copy-start.1 = (f32[16,60,16]{0,1,2:T(8,128)S(1)}, f32[16,60,16]{0,1,2:T(8,128)}, u32[]{:S(2)}) copy-start(f32[16,60,16]{0,1,2:T(8,128)} %copy-done) | copy-start | bytes 184324
  649.9 17.4 %copy-start.78 = (pred[16]{0:T(512)(128)(4,1)S(1)}, pred[16]{0:T(512)(128)(4,1)}, u32[]{:S(2)}) copy-start(pred[16]{0:T(512)(128)(4,1)} %get-tuple-element.437) | copy-start | bytes 52
  708.1 79.8 %copy-start.10 = (f32[16,60,16]{0,1,2:T(8,128)}, f32[16,60,16]{0,1,2:T(8,128)S(1)}, u32[]{:S(2)}) copy-start(f32[16,60,16]{0,1,2:T(8,128)S(1)} %copy.526) | copy-start | bytes 184324
  1134.5 18.0 %copy-start.17 = (f32[16,60,16]{1,2,0:T(8,128)S(1)}, f32[16,60,16]{1,2,0:T(8,128)}, u32[]{:S(2)}) copy-start(f32[16,60,16]{1,2,0:T(8,128)} %gather_fusion.13) | copy-start | bytes 184324
  1137.2 33.4 %collective-permute-start.2 = (f32[1,2,60,256]{2,3,1,0:T(8,128)}, f32[1,2,60,256]{2,3,1,0:T(8,128)}, u32[]{:S(2)}, u32[]{:S(2)}) collective-permute-start(f32[1,2,60,256]{2,3,1,0:T(8,128)} %pad_maximum_fusion.4), channel_id=1, source_target_pairs={{0,8},{8,16},{16,24},{24,32},{32,40},{40,48},{48,56},{56,64},{64,7... | collective-permute-start | bytes 368648 | tf_op jit(solution)/shard_map/ppermute | solution.py:29
  1139.1 22.2 %copy-start.51 = (f32[128,128]{1,0:T(8,128)S(1)}, f32[128,128]{1,0:T(8,128)}, u32[]{:S(2)}) copy-start(f32[128,128]{1,0:T(8,128)} %constant.210.clone) | copy-start | bytes 196612
  1139.1 35.8 %collective-permute-start.3 = (f32[1,2,60,256]{2,3,1,0:T(8,128)}, f32[1,2,60,256]{2,3,1,0:T(8,128)}, u32[]{:S(2)}, u32[]{:S(2)}) collective-permute-start(f32[1,2,60,256]{2,3,1,0:T(8,128)} %pad_maximum_fusion.5), channel_id=1, source_target_pairs={{8,0},{16,8},{24,16},{32,24},{40,32},{48,40},{56,48},{64,56},{72,6... | collective-permute-start | bytes 368648 | tf_op jit(solution)/shard_map/ppermute | solution.py:32
  1147.1 17.6 %copy-start.11 = (f32[16,60,16]{0,1,2:T(8,128)S(1)}, f32[16,60,16]{0,1,2:T(8,128)}, u32[]{:S(2)}) copy-start(f32[16,60,16]{0,1,2:T(8,128)} %copy-done.10) | copy-start | bytes 184324
  1147.1 17.6 %copy-start.13 = (f32[16,60,16]{0,1,2:T(8,128)S(1)}, f32[16,60,16]{0,1,2:T(8,128)}, u32[]{:S(2)}) copy-start(f32[16,60,16]{0,1,2:T(8,128)} %copy-done.12) | copy-start | bytes 184324
  1147.1 17.6 %copy-start.77 = (pred[16]{0:T(512)(128)(4,1)S(1)}, pred[16]{0:T(512)(128)(4,1)}, u32[]{:S(2)}) copy-start(pred[16]{0:T(512)(128)(4,1)} %get-tuple-element.435) | copy-start | bytes 52
  1147.1 17.6 %copy-start.79 = (pred[16]{0:T(512)(128)(4,1)S(1)}, pred[16]{0:T(512)(128)(4,1)}, u32[]{:S(2)}) copy-start(pred[16]{0:T(512)(128)(4,1)} %get-tuple-element.437) | copy-start | bytes 52
  (61 other events, 391.7 us)
Sparse Core Ops, SparseCore 0:
  10.5 81.7 all-gather.5
  94.0 84.4 all-gather.3
  180.8 89.9 reduce-scatter.1
  697.4 88.1 all-gather.7
where the time goes:
time: 1210 us; the launch traced here: 1200 us
  local copies, waits for them, and re-layouts  474 us (39%)
  waiting for transfers between devices  271 us (22%)
  other arithmetic  243 us (20%)
  matrix products  160 us (13%)
  blocking collectives  22.7 us (2%)
  between operations  18 us (1%)
    convert_element_type x20, local copies, waits for them, and re-layouts, one_slab(): expanded = (picked.astype(jnp.float32)[:, :, :, None, :] * spread[None, N...  315 us
    convert_element_type x20, other arithmetic, one_slab(): expanded = (picked.astype(jnp.float32)[:, :, :, None, :] * spread[None, N...  189 us
    dot_general x20, matrix products, one_slab(): jnp.einsum('bil,bcln->cbin', weights, expanded, preferred_element_type=jn...  142 us
    all_gather x2, waiting for transfers between devices, apply_jacobian(): gathered = lax.all_gather(gradients, 'mode', axis=1, tiled=True)  134 us
    reduce_scatter x1, waiting for transfers between devices, per_device(): lax.psum_scatter(lax.dot_general(low_state, local_basis, (((0,), (1,)), (...  86.9 us
    all_gather x1, waiting for transfers between devices, apply_jacobian(): lax.all_gather(triple_blocks, 'elem', axis=2, tiled=True)  49.8 us
    unnamed x174, local copies, waits for them, and re-layouts  29.8 us
  transfers between devices with their start and end apart: 8, of which 4 were waited for; matrix products, arithmetic and copies ran while one was open for 12% of the time, Pallas kernels for 0%

commit v1 on v0

--- a/solution.py
+++ b/solution.py
@@ -169,7 +169,10 @@
     gradients = jnp.stack([volume_derivative(iterate_now, single) for single in tables]).astype(
         jnp.bfloat16
     )
-    gathered = lax.all_gather(gradients, "mode", axis=1, tiled=True)
+    count_2 = lax.axis_size("mode")
+    blocks = jnp.stack([gradients for _ in range(count_2)])
+    blocks = lax.all_to_all(blocks, "mode", split_axis=0, concat_axis=0)
+    gathered = jnp.concatenate(blocks, axis=1)
     selected = select_blocks(gathered, block_columns)
     empty_sum = jnp.zeros((3, block_columns.shape[0], MB, nodes_count), jnp.float32)
     running = add_slab(

time: 1210 us -> 1080 us (0.89)
  waiting for transfers between devices: 271 us -> 117 us
  starting transfers between devices: 6.18 us -> 20.3 us
    all_gather x2 -> x0, waiting for transfers between devices: 134 us -> none  [apply_jacobian(): gathered = lax.all_gather(gradients, 'mode', axis=1, tiled=True)]
    reduce_scatter x1, waiting for transfers between devices: 86.9 us -> 0.01 us  [per_device(): lax.psum_scatter(lax.dot_general(low_state, local_basis, (((0,), (1,)), (...]
    all_to_all x0 -> x2, waiting for transfers between devices: none -> 53.8 us  [apply_jacobian(): blocks = lax.all_to_all(blocks, 'mode', split_axis=0, concat_axis=0)]
    reshape x0 -> x4, local copies, waits for them, and re-layouts: none -> 16.8 us  [apply_jacobian(): gathered = jnp.concatenate(blocks, axis=1)]
    all_to_all x0 -> x2, starting transfers between devices: none -> 14 us  [apply_jacobian(): blocks = lax.all_to_all(blocks, 'mode', split_axis=0, concat_axis=0)]
    all_gather x1, waiting for transfers between devices: 49.8 us -> 62.9 us  [apply_jacobian(): lax.all_gather(triple_blocks, 'elem', axis=2, tiled=True)]
    unnamed x174 -> x214, local copies, waits for them, and re-layouts: 29.8 us -> 26.6 us
  transfers between devices with their start and end apart: 8 -> 8, of which waited for: 4 -> 3; matrix products, arithmetic and copies ran while one was open for 12% -> 13% of each run, Pallas kernels for 0% -> 0%
where the time goes in v1:
time: 1080 us; the launch traced here: 1060 us
  local copies, waits for them, and re-layouts  481 us (45%)
  other arithmetic  236 us (22%)
  matrix products  161 us (15%)
  waiting for transfers between devices  117 us (11%)
  blocking collectives  22.8 us (2%)
  starting transfers between devices  20.3 us (2%)
  between operations  20 us (2%)
    convert_element_type x20, local copies, waits for them, and re-layouts, one_slab(): expanded = (picked.astype(jnp.float32)[:, :, :, None, :] * spread[None, N...  310 us
    convert_element_type x20, other arithmetic, one_slab(): expanded = (picked.astype(jnp.float32)[:, :, :, None, :] * spread[None, N...  189 us
    dot_general x20, matrix products, one_slab(): jnp.einsum('bil,bcln->cbin', weights, expanded, preferred_element_type=jn...  142 us
    all_gather x1, waiting for transfers between devices, apply_jacobian(): lax.all_gather(triple_blocks, 'elem', axis=2, tiled=True)  62.9 us
    all_to_all x2, waiting for transfers between devices, apply_jacobian(): blocks = lax.all_to_all(blocks, 'mode', split_axis=0, concat_axis=0)  53.8 us
    unnamed x214, local copies, waits for them, and re-layouts  26.6 us
    all_gather x1, blocking collectives, per_device(): lax.all_gather(node_terms.T.astype(jnp.bfloat16), 'mode', axis=1, tiled=T...  22.8 us
  transfers between devices with their start and end apart: 8, of which 3 were waited for; matrix products, arithmetic and copies ran while one was open for 13% of the time, Pallas kernels for 0%

profile of v1, /device:TPU:34, one launch (start us, length us, event | category | flops | bytes accessed | tf_op | source)
XLA Modules:
  0.0 1058.3 jit_solution(16838757615371968246)
XLA Ops:
  49.7 29.6 %all-to-all-done = bf16[8,3,60,1024]{3,2,1,0:T(8,128)(2,1)} async-done(((bf16[8,3,60,1024]{3,2,1,0:T(8,128)(2,1)}), bf16[8,3,60,1024]{3,2,1,0:T(8,128)(2,1)}, u32[]{:S(2)}, u32[]{:S(2)}) %all-to-all-start) | async-done | bytes 2949152 | tf_op jit(solution)/shard_map/all_to_all | solution.py:174
  91.1 62.9 %all-gather.2.cloned.1.call-done = bf16[1,60,20160]{1,0,2:T(2,128)(2,1)} async-done(((bf16[1,60,1260]{1,0,2:T(2,128)(2,1)}), bf16[1,60,20160]{1,0,2:T(2,128)(2,1)}) %all-gather.2.cloned.1.call-update) | async-done | bytes 2419216 | tf_op jit(solution)/shard_map/all_gather | solution.py:180
  154.0 20.8 %copy.454 = bf16[1,60,20160]{2,1,0:T(8,128)(2,1)} copy(bf16[1,60,20160]{1,0,2:T(2,128)(2,1)} %all-gather.2.cloned.1.call-done) | data formatting | bytes 4838400
  176.3 22.8 %all_gather.7 = bf16[84,1024]{1,0:T(8,128)(2,1)S(1)} all-gather(bf16[84,128]{1,0:T(8,128)(2,1)S(1)} %fusion.9), channel_id=1, replica_groups=mesh['elem'=16,'mode'=8] {'mode'}, dimensions={1}, use_global_device_ids=true | all-gather | bytes 193536 | tf_op jit(solution)/shard_map/all_gather | solution.py:238
  199.2 330.1 %while.32 = (s32[]{:T(128)}, f32[3,1,60,1024]{3,2,0,1:T(8,128)S(1)}, bf16[1,3,240,1024]{3,2,1,0:T(8,128)(2,1)}, f32[84,1024]{1,0:T(8,128)S(1)}, bf16[1,60,20160]...) while((s32[]{:T(128)}, ...), condition=%wide.region_2.3_spmd.clone, body=%wide.region_1.2_spmd.clone.sunk | while | flops 756006912 | bytes 52363480 | solution.py:162
  200.2 9.4 multiply_convert_fusion.4
  209.6 15.5 %convert_element_type.118 = bf16[3,2016,1024]{2,1,0:T(8,128)(2,1)} reshape(bf16[3,24,84,1024]{3,2,1,0:T(8,128)(2,1)} %multiply_convert_fusion.4) | data formatting | bytes 24772608 | tf_op jit(solution)/shard_map/while/body/eval_jaxpr/convert_element_type | solution.py:155
  242.6 15.5 %convert_element_type.118 = bf16[3,2016,1024]{2,1,0:T(8,128)(2,1)} reshape(bf16[3,24,84,1024]{3,2,1,0:T(8,128)(2,1)} %multiply_convert_fusion.4) | data formatting | bytes 24772608 | tf_op jit(solution)/shard_map/while/body/eval_jaxpr/convert_element_type | solution.py:155
  266.2 9.4 multiply_convert_fusion.4
  275.6 15.5 %convert_element_type.118 = bf16[3,2016,1024]{2,1,0:T(8,128)(2,1)} reshape(bf16[3,24,84,1024]{3,2,1,0:T(8,128)(2,1)} %multiply_convert_fusion.4) | data formatting | bytes 24772608 | tf_op jit(solution)/shard_map/while/body/eval_jaxpr/convert_element_type | solution.py:155
  299.2 9.4 multiply_convert_fusion.4
  308.6 15.5 %convert_element_type.118 = bf16[3,2016,1024]{2,1,0:T(8,128)(2,1)} reshape(bf16[3,24,84,1024]{3,2,1,0:T(8,128)(2,1)} %multiply_convert_fusion.4) | data formatting | bytes 24772608 | tf_op jit(solution)/shard_map/while/body/eval_jaxpr/convert_element_type | solution.py:155
  332.2 9.4 multiply_convert_fusion.4
  341.6 15.5 %convert_element_type.118 = bf16[3,2016,1024]{2,1,0:T(8,128)(2,1)} reshape(bf16[3,24,84,1024]{3,2,1,0:T(8,128)(2,1)} %multiply_convert_fusion.4) | data formatting | bytes 24772608 | tf_op jit(solution)/shard_map/while/body/eval_jaxpr/convert_element_type | solution.py:155
  365.2 9.4 multiply_convert_fusion.4
  374.6 15.5 %convert_element_type.118 = bf16[3,2016,1024]{2,1,0:T(8,128)(2,1)} reshape(bf16[3,24,84,1024]{3,2,1,0:T(8,128)(2,1)} %multiply_convert_fusion.4) | data formatting | bytes 24772608 | tf_op jit(solution)/shard_map/while/body/eval_jaxpr/convert_element_type | solution.py:155
  407.6 15.5 %convert_element_type.118 = bf16[3,2016,1024]{2,1,0:T(8,128)(2,1)} reshape(bf16[3,24,84,1024]{3,2,1,0:T(8,128)(2,1)} %multiply_convert_fusion.4) | data formatting | bytes 24772608 | tf_op jit(solution)/shard_map/while/body/eval_jaxpr/convert_element_type | solution.py:155
  440.6 15.5 %convert_element_type.118 = bf16[3,2016,1024]{2,1,0:T(8,128)(2,1)} reshape(bf16[3,24,84,1024]{3,2,1,0:T(8,128)(2,1)} %multiply_convert_fusion.4) | data formatting | bytes 24772608 | tf_op jit(solution)/shard_map/while/body/eval_jaxpr/convert_element_type | solution.py:155
  473.6 15.5 %convert_element_type.118 = bf16[3,2016,1024]{2,1,0:T(8,128)(2,1)} reshape(bf16[3,24,84,1024]{3,2,1,0:T(8,128)(2,1)} %multiply_convert_fusion.4) | data formatting | bytes 24772608 | tf_op jit(solution)/shard_map/while/body/eval_jaxpr/convert_element_type | solution.py:155
  506.7 15.5 %convert_element_type.118 = bf16[3,2016,1024]{2,1,0:T(8,128)(2,1)} reshape(bf16[3,24,84,1024]{3,2,1,0:T(8,128)(2,1)} %multiply_convert_fusion.4) | data formatting | bytes 24772608 | tf_op jit(solution)/shard_map/while/body/eval_jaxpr/convert_element_type | solution.py:155
  621.9 24.2 %all-to-all-done.1 = bf16[8,3,60,1024]{3,2,1,0:T(8,128)(2,1)} async-done(((bf16[8,3,60,1024]{3,2,1,0:T(8,128)(2,1)}), bf16[8,3,60,1024]{3,2,1,0:T(8,128)(2,1)}, u32[]{:S(2)}, u32[]{:S(2)}) %all-to-all-start.1) | async-done | bytes 2949152 | tf_op jit(solution)/shard_map/all_to_all | solution.py:174
  657.9 330.1 %while.33 = (s32[]{:T(128)}, f32[3,1,60,1024]{3,2,0,1:T(8,128)S(1)}, bf16[1,3,240,1024]{3,2,1,0:T(8,128)(2,1)}, f32[84,1024]{1,0:T(8,128)S(1)}, bf16[1,60,20160]...) while((s32[]{:T(128)}, ...), condition=%wide.region_4.6_spmd.clone, body=%wide.region_3.5_spmd.clone.sunk | while | flops 756006912 | bytes 52363480 | solution.py:162
  668.2 15.5 %convert_element_type.120 = bf16[3,2016,1024]{2,1,0:T(8,128)(2,1)} reshape(bf16[3,24,84,1024]{3,2,1,0:T(8,128)(2,1)} %multiply_convert_fusion.5) | data formatting | bytes 24772608 | tf_op jit(solution)/shard_map/while/body/eval_jaxpr/convert_element_type | solution.py:155
  701.3 15.5 %convert_element_type.120 = bf16[3,2016,1024]{2,1,0:T(8,128)(2,1)} reshape(bf16[3,24,84,1024]{3,2,1,0:T(8,128)(2,1)} %multiply_convert_fusion.5) | data formatting | bytes 24772608 | tf_op jit(solution)/shard_map/while/body/eval_jaxpr/convert_element_type | solution.py:155
  734.3 15.5 %convert_element_type.120 = bf16[3,2016,1024]{2,1,0:T(8,128)(2,1)} reshape(bf16[3,24,84,1024]{3,2,1,0:T(8,128)(2,1)} %multiply_convert_fusion.5) | data formatting | bytes 24772608 | tf_op jit(solution)/shard_map/while/body/eval_jaxpr/convert_element_type | solution.py:155
  767.2 15.5 %convert_element_type.120 = bf16[3,2016,1024]{2,1,0:T(8,128)(2,1)} reshape(bf16[3,24,84,1024]{3,2,1,0:T(8,128)(2,1)} %multiply_convert_fusion.5) | data formatting | bytes 24772608 | tf_op jit(solution)/shard_map/while/body/eval_jaxpr/convert_element_type | solution.py:155
  800.3 15.5 %convert_element_type.120 = bf16[3,2016,1024]{2,1,0:T(8,128)(2,1)} reshape(bf16[3,24,84,1024]{3,2,1,0:T(8,128)(2,1)} %multiply_convert_fusion.5) | data formatting | bytes 24772608 | tf_op jit(solution)/shard_map/while/body/eval_jaxpr/convert_element_type | solution.py:155
  833.3 15.5 %convert_element_type.120 = bf16[3,2016,1024]{2,1,0:T(8,128)(2,1)} reshape(bf16[3,24,84,1024]{3,2,1,0:T(8,128)(2,1)} %multiply_convert_fusion.5) | data formatting | bytes 24772608 | tf_op jit(solution)/shard_map/while/body/eval_jaxpr/convert_element_type | solution.py:155
  866.3 15.5 %convert_element_type.120 = bf16[3,2016,1024]{2,1,0:T(8,128)(2,1)} reshape(bf16[3,24,84,1024]{3,2,1,0:T(8,128)(2,1)} %multiply_convert_fusion.5) | data formatting | bytes 24772608 | tf_op jit(solution)/shard_map/while/body/eval_jaxpr/convert_element_type | solution.py:155
  899.3 15.5 %convert_element_type.120 = bf16[3,2016,1024]{2,1,0:T(8,128)(2,1)} reshape(bf16[3,24,84,1024]{3,2,1,0:T(8,128)(2,1)} %multiply_convert_fusion.5) | data formatting | bytes 24772608 | tf_op jit(solution)/shard_map/while/body/eval_jaxpr/convert_element_type | solution.py:155
  932.3 15.5 %convert_element_type.120 = bf16[3,2016,1024]{2,1,0:T(8,128)(2,1)} reshape(bf16[3,24,84,1024]{3,2,1,0:T(8,128)(2,1)} %multiply_convert_fusion.5) | data formatting | bytes 24772608 | tf_op jit(solution)/shard_map/while/body/eval_jaxpr/convert_element_type | solution.py:155
  965.3 15.5 %convert_element_type.120 = bf16[3,2016,1024]{2,1,0:T(8,128)(2,1)} reshape(bf16[3,24,84,1024]{3,2,1,0:T(8,128)(2,1)} %multiply_convert_fusion.5) | data formatting | bytes 24772608 | tf_op jit(solution)/shard_map/while/body/eval_jaxpr/convert_element_type | solution.py:155
  (497 shorter events, 520.4 us)
Async XLA Ops:
  8.0 146.0 %all-gather.2.cloned.1.call-start = ((), (), s32[]{:S(2)}) async-start(), calls=%async_computation.4 | async-start | bytes 10967040 | tf_op jit(solution)/shard_map/all_gather | solution.py:180
  10.2 164.7 %reduce-scatter.2.cloned.1.call-start = ((), (), s32[]{:S(2)}) async-start(), calls=%async_computation.3 | async-start | bytes 4718592 | tf_op jit(solution)/shard_map/reduce_scatter | solution.py:227
  20.4 58.9 %all-to-all-start = ((bf16[8,3,60,1024]{3,2,1,0:T(8,128)(2,1)}), bf16[8,3,60,1024]{3,2,1,0:T(8,128)(2,1)}, u32[]{:S(2)}, u32[]{:S(2)}) async-start(bf16[8,3,60,1024]{3,2,1,0:T(8,128)(2,1)} %stack.92), calls=%async_computation | async-start | bytes 6291456 | tf_op jit(solution)/shard_map/all_to_all | solution.py:174
  33.1 498.2 %copy-start.81 = (s32[1024]{0:T(1024)}, s32[1024]{0:T(1024)S(1)}, u32[]{:S(2)}) copy-start(s32[1024]{0:T(1024)S(1)} %pad_clamp_fusion.3) | copy-start | bytes 12292
  35.5 497.9 %copy-start.80 = (s32[1024]{0:T(1024)}, s32[1024]{0:T(1024)S(1)}, u32[]{:S(2)}) copy-start(s32[1024]{0:T(1024)S(1)} %pad_clamp_fusion.5) | copy-start | bytes 12292
  36.4 497.6 %copy-start.83 = (s32[1024]{0:T(1024)}, s32[1024]{0:T(1024)S(1)}, u32[]{:S(2)}) copy-start(s32[1024]{0:T(1024)S(1)} %pad_clamp_fusion.7) | copy-start | bytes 12292
  39.7 499.4 %copy-start.84 = (s32[1024]{0:T(1024)}, s32[1024]{0:T(1024)S(1)}, u32[]{:S(2)}) copy-start(s32[1024]{0:T(1024)S(1)} %pad_clamp_fusion.11) | copy-start | bytes 12292
  42.0 527.0 %copy-start.93 = (pred[16]{0:T(512)(128)(4,1)}, pred[16]{0:T(512)(128)(4,1)S(1)}, u32[]{:S(2)}) copy-start(pred[16]{0:T(512)(128)(4,1)S(1)} %get-tuple-element.439) | copy-start | bytes 52
  42.0 528.0 %copy-start.95 = (pred[16]{0:T(512)(128)(4,1)}, pred[16]{0:T(512)(128)(4,1)S(1)}, u32[]{:S(2)}) copy-start(pred[16]{0:T(512)(128)(4,1)S(1)} %get-tuple-element.441) | copy-start | bytes 52
  42.0 538.5 %copy-start.89 = (pred[16]{0:T(512)(128)(4,1)}, pred[16]{0:T(512)(128)(4,1)S(1)}, u32[]{:S(2)}) copy-start(pred[16]{0:T(512)(128)(4,1)S(1)} %get-tuple-element.395) | copy-start | bytes 52
  42.0 541.1 %copy-start.91 = (pred[16]{0:T(512)(128)(4,1)}, pred[16]{0:T(512)(128)(4,1)S(1)}, u32[]{:S(2)}) copy-start(pred[16]{0:T(512)(128)(4,1)S(1)} %get-tuple-element.443) | copy-start | bytes 52
  42.0 503.8 %copy-start.86 = (s32[1024]{0:T(1024)}, s32[1024]{0:T(1024)S(1)}, u32[]{:S(2)}) copy-start(s32[1024]{0:T(1024)S(1)} %pad_clamp_fusion.4) | copy-start | bytes 12292
  43.4 504.1 %copy-start.85 = (s32[1024]{0:T(1024)}, s32[1024]{0:T(1024)S(1)}, u32[]{:S(2)}) copy-start(s32[1024]{0:T(1024)S(1)} %pad_clamp_fusion.6) | copy-start | bytes 12292
  45.8 504.1 %copy-start.82 = (s32[1024]{0:T(1024)}, s32[1024]{0:T(1024)S(1)}, u32[]{:S(2)}) copy-start(s32[1024]{0:T(1024)S(1)} %pad_clamp_fusion.8) | copy-start | bytes 12292
  47.2 504.4 %copy-start.87 = (s32[1024]{0:T(1024)}, s32[1024]{0:T(1024)S(1)}, u32[]{:S(2)}) copy-start(s32[1024]{0:T(1024)S(1)} %pad_clamp_fusion.10) | copy-start | bytes 12292
  542.9 29.1 %collective-permute-start.1 = (f32[1,2,60,256]{2,3,1,0:T(8,128)}, f32[1,2,60,256]{2,3,1,0:T(8,128)}, u32[]{:S(2)}, u32[]{:S(2)}) collective-permute-start(f32[1,2,60,256]{2,3,1,0:T(8,128)} %pad_maximum_fusion.3), channel_id=1, source_target_pairs={{8,0},{16,8},{24,16},{32,24},{40,32},{48,40},{56,48},{64,56},{72,6... | collective-permute-start | bytes 368648 | tf_op jit(solution)/shard_map/ppermute | solution.py:32
  544.8 31.5 %collective-permute-start = (f32[1,2,60,256]{2,3,1,0:T(8,128)}, f32[1,2,60,256]{2,3,1,0:T(8,128)}, u32[]{:S(2)}, u32[]{:S(2)}) collective-permute-start(f32[1,2,60,256]{2,3,1,0:T(8,128)} %pad_maximum_fusion.2), channel_id=1, source_target_pairs={{0,8},{8,16},{16,24},{24,32},{32,40},{40,48},{48,56},{56,64},{64,7... | collective-permute-start | bytes 368648 | tf_op jit(solution)/shard_map/ppermute | solution.py:29
  547.5 12.4 %copy-start.64 = (f32[128,128]{1,0:T(8,128)S(1)}, f32[128,128]{1,0:T(8,128)}, u32[]{:S(2)}) copy-start(f32[128,128]{1,0:T(8,128)} %constant.210.clone) | copy-start | bytes 196612
  549.6 14.5 %copy-start.4 = (f32[16,60,16]{0,1,2:T(8,128)S(1)}, f32[16,60,16]{0,1,2:T(8,128)}, u32[]{:S(2)}) copy-start(f32[16,60,16]{0,1,2:T(8,128)} %copy.468) | copy-start | bytes 184324
  549.6 14.5 %copy-start.97 = (pred[16]{0:T(512)(128)(4,1)S(1)}, pred[16]{0:T(512)(128)(4,1)}, u32[]{:S(2)}) copy-start(pred[16]{0:T(512)(128)(4,1)} %get-tuple-element.435) | copy-start | bytes 52
  551.6 15.1 %copy-start.1 = (f32[16,60,16]{0,1,2:T(8,128)S(1)}, f32[16,60,16]{0,1,2:T(8,128)}, u32[]{:S(2)}) copy-start(f32[16,60,16]{0,1,2:T(8,128)} %copy-done) | copy-start | bytes 184324
  551.6 15.1 %copy-start.99 = (pred[16]{0:T(512)(128)(4,1)S(1)}, pred[16]{0:T(512)(128)(4,1)}, u32[]{:S(2)}) copy-start(pred[16]{0:T(512)(128)(4,1)} %get-tuple-element.437) | copy-start | bytes 52
  595.2 51.0 %all-to-all-start.1 = ((bf16[8,3,60,1024]{3,2,1,0:T(8,128)(2,1)}), bf16[8,3,60,1024]{3,2,1,0:T(8,128)(2,1)}, u32[]{:S(2)}, u32[]{:S(2)}) async-start(bf16[8,3,60,1024]{3,2,1,0:T(8,128)(2,1)} %stack.104), calls=%async_computation.2 | async-start | bytes 6291456 | tf_op jit(solution)/shard_map/all_to_all | solution.py:174
  999.1 13.7 %copy-start.21 = (f32[16,60,16]{1,2,0:T(8,128)S(1)}, f32[16,60,16]{1,2,0:T(8,128)}, u32[]{:S(2)}) copy-start(f32[16,60,16]{1,2,0:T(8,128)} %gather_fusion.12) | copy-start | bytes 184324
  1000.9 32.0 %collective-permute-start.2 = (f32[1,2,60,256]{2,3,1,0:T(8,128)}, f32[1,2,60,256]{2,3,1,0:T(8,128)}, u32[]{:S(2)}, u32[]{:S(2)}) collective-permute-start(f32[1,2,60,256]{2,3,1,0:T(8,128)} %pad_maximum_fusion.4), channel_id=1, source_target_pairs={{0,8},{8,16},{16,24},{24,32},{32,40},{40,48},{48,56},{56,64},{64,7... | collective-permute-start | bytes 368648 | tf_op jit(solution)/shard_map/ppermute | solution.py:29
  1002.0 12.7 %copy-start.20 = (f32[16,60,16]{1,2,0:T(8,128)S(1)}, f32[16,60,16]{1,2,0:T(8,128)}, u32[]{:S(2)}) copy-start(f32[16,60,16]{1,2,0:T(8,128)} %gather_fusion.13) | copy-start | bytes 184324
  1002.8 34.5 %collective-permute-start.3 = (f32[1,2,60,256]{2,3,1,0:T(8,128)}, f32[1,2,60,256]{2,3,1,0:T(8,128)}, u32[]{:S(2)}, u32[]{:S(2)}) collective-permute-start(f32[1,2,60,256]{2,3,1,0:T(8,128)} %pad_maximum_fusion.5), channel_id=1, source_target_pairs={{8,0},{16,8},{24,16},{32,24},{40,32},{48,40},{56,48},{64,56},{72,6... | collective-permute-start | bytes 368648 | tf_op jit(solution)/shard_map/ppermute | solution.py:32
  1010.5 13.0 %copy-start.66 = (f32[128,128]{1,0:T(8,128)S(1)}, f32[128,128]{1,0:T(8,128)}, u32[]{:S(2)}) copy-start(f32[128,128]{1,0:T(8,128)} %constant.210.clone) | copy-start | bytes 196612
  1012.8 14.3 %copy-start.14 = (f32[16,60,16]{0,1,2:T(8,128)S(1)}, f32[16,60,16]{0,1,2:T(8,128)}, u32[]{:S(2)}) copy-start(f32[16,60,16]{0,1,2:T(8,128)} %copy-done.13) | copy-start | bytes 184324
  1012.8 14.3 %copy-start.16 = (f32[16,60,16]{0,1,2:T(8,128)S(1)}, f32[16,60,16]{0,1,2:T(8,128)}, u32[]{:S(2)}) copy-start(f32[16,60,16]{0,1,2:T(8,128)} %copy-done.15) | copy-start | bytes 184324
  1012.8 14.3 %copy-start.98 = (pred[16]{0:T(512)(128)(4,1)S(1)}, pred[16]{0:T(512)(128)(4,1)}, u32[]{:S(2)}) copy-start(pred[16]{0:T(512)(128)(4,1)} %get-tuple-element.435) | copy-start | bytes 52
  1012.8 14.3 %copy-start.100 = (pred[16]{0:T(512)(128)(4,1)S(1)}, pred[16]{0:T(512)(128)(4,1)}, u32[]{:S(2)}) copy-start(pred[16]{0:T(512)(128)(4,1)} %get-tuple-element.437) | copy-start | bytes 52
  (82 other events, 358.1 us)
Sparse Core Ops, SparseCore 0:
  11.3 142.6 all-gather.1
Sparse Core Ops, SparseCore 1:
  14.1 159.3 reduce-scatter.1
